TPU v7x, 256 devices: a whole 4x4x8 slice. The times are simulated.
256 devices in a mesh: dp: 8 (over x, y_hi), seq: 32 (over y_lo, z, core).
Axes of the slice: x: 4, y: 4 (y_hi: 2, y_lo: 2; y = y_hi * 2 + y_lo), z: 8, core: 2. Of those that a mesh axis runs over, the one named last changes fastest.
Arguments:
- inputs: bfloat16 [8, 16384, 1024], P('dp', 'seq'), may hold values from -6 to 6
- out_grad: bfloat16 [8, 16384, 1024], P('dp', 'seq'), may hold values from -6 to 6
- w_in: bfloat16 [1024, 3072], replicated, may hold values from -0.1875 to 0.1875
- taps: float32 [3, 3072], replicated, may hold values from -3 to 3
- filt: bfloat16 [64, 256, 1024], P(None, 'seq'), may hold values from -4 to 4
Outputs:
- mixed: bfloat16 [8, 16384, 1024], P('dp', 'seq')
- in_grad: bfloat16 [8, 16384, 1024], P('dp', 'seq')
- w_in_grad: float32 [1024, 3072], P('dp', 'seq')
- taps_grad: float32 [3, 3072], replicated
All inputs are finite; a program needn't handle non-finite values.
Results may differ from a plain program's by a relative error of at most 0.012.
Values may be sent and summed in bfloat16 or wider, within the bound.
A program may use at most 128 MiB of HBM per device.

v0:
```python
import math

import jax
import jax.numpy as jnp
from jax import lax
from jax.sharding import PartitionSpec as P

BLK = 256


def padded(cells, sides, width):
    for axis, dim in sides:
        count = lax.axis_size(axis)
        ends = count - 1
        head = lax.slice_in_dim(cells, 0, width, axis=dim)
        tail = lax.slice_in_dim(cells, cells.shape[dim] - width, cells.shape[dim], axis=dim)
        cells = jnp.concatenate(
            [
                lax.ppermute(tail, axis, [(i, (i + 1) % count) for i in range(ends)]),
                cells,
                lax.ppermute(head, axis, [((i + 1) % count, i) for i in range(ends)]),
            ],
            axis=dim,
        )
    return cells


def dct_table(count):
    rows = jnp.arange(count, dtype=jnp.float32)[:, None]
    cols = jnp.arange(count, dtype=jnp.float32)[None, :]
    first = jnp.where(rows == 0, jnp.float32(math.sqrt(0.5)), jnp.float32(1.0))
    table = (
        jnp.float32(math.sqrt(2.0 / count))
        * first
        * jnp.cos(jnp.float32(math.pi) * (cols + 0.5) * rows / count)
    )
    return table.astype(jnp.bfloat16)


def block_section(blocks, table_q):
    return jnp.einsum("rq,nbqd->nbrd", table_q, blocks, preferred_element_type=jnp.float32).astype(
        jnp.bfloat16
    )


def span_section(columns, filt, table_p):
    stack, span, narrow, width = columns.shape
    flat = columns.reshape(stack, span, narrow * width)
    second = jnp.einsum("ap,npk->nak", table_p, flat, preferred_element_type=jnp.float32)
    scaled = (filt.reshape(1, span, narrow * width).astype(jnp.float32) * second).astype(
        jnp.bfloat16
    )
    third = jnp.einsum("ap,nak->npk", table_p, scaled, preferred_element_type=jnp.float32).astype(
        jnp.bfloat16
    )
    return third.reshape(columns.shape)


def final_section(blocks, table_q):
    return jnp.einsum("rq,nbrd->nbqd", table_q, blocks, preferred_element_type=jnp.float32)


def shards(inputs, out_grad, w_in, taps, filt):
    tok = inputs.shape[1]
    width = inputs.shape[2]
    nseq = lax.axis_size("seq")
    ndata = lax.axis_size("dp")
    nblocks = tok // BLK
    table_q = dct_table(BLK)
    table_p = dct_table(filt.shape[0])
    factor = 1.0 / math.sqrt(ndata * nseq * tok)
    rows = inputs[0]
    z = jnp.dot(rows, w_in, preferred_element_type=jnp.float32).astype(jnp.bfloat16)
    zpad = padded(z, (("seq", 0),), 1)
    s = taps[0] * zpad[:-2] + taps[1] * zpad[1:-1] + taps[2] * zpad[2:]
    a_part = s[:, :width]
    g_part = s[:, width : 2 * width]
    v_part = s[:, 2 * width :]
    w = (a_part * v_part).astype(jnp.bfloat16)
    gradf = out_grad[0].astype(jnp.float32)
    e4 = (gradf * g_part).astype(jnp.bfloat16)
    columns = lax.all_to_all(
        block_section(w.reshape(1, nblocks, BLK, width), table_q),
        "seq",
        split_axis=2,
        concat_axis=1,
        tiled=True,
    )
    back = lax.all_to_all(
        span_section(columns, filt, table_p), "seq", split_axis=1, concat_axis=2, tiled=True
    )
    h4 = final_section(back, table_q).reshape(tok, width)
    grad_cols = lax.all_to_all(
        block_section(e4.reshape(1, nblocks, BLK, width), table_q),
        "seq",
        split_axis=2,
        concat_axis=1,
        tiled=True,
    )
    grad_back = lax.all_to_all(
        span_section(grad_cols, filt, table_p), "seq", split_axis=1, concat_axis=2, tiled=True
    )
    dw = final_section(grad_back, table_q).reshape(tok, width)
    mixed = (g_part * h4).astype(jnp.bfloat16)
    ds = jnp.concatenate([dw * v_part, gradf * h4, dw * a_part], axis=1).astype(jnp.bfloat16)
    dspad = padded(ds, (("seq", 0),), 1)
    du = (taps[0] * dspad[2:] + taps[1] * dspad[1:-1] + taps[2] * dspad[:-2]).astype(jnp.bfloat16)
    in_grad = jnp.dot(du, w_in.T, preferred_element_type=jnp.float32).astype(jnp.bfloat16)
    dsf = ds.astype(jnp.float32)
    zf = zpad.astype(jnp.float32)
    local_taps = jnp.stack([jnp.sum(dsf * zf[k : k + tok], axis=0) for k in range(3)])
    taps_grad = lax.psum(local_taps, ("dp", "seq")) * factor
    contract = (((0,), (0,)), ((), ()))
    partial_sum = lax.psum_scatter(
        lax.dot_general(rows, du, contract, preferred_element_type=jnp.float32),
        "dp",
        scatter_dimension=0,
        tiled=True,
    )
    w_grad = lax.psum_scatter(partial_sum, "seq", scatter_dimension=1, tiled=True) * factor
    return (mixed[None], in_grad[None], w_grad, taps_grad)


def solution(mesh):
    return jax.shard_map(
        shards,
        mesh=mesh,
        in_specs=(P("dp", "seq", None), P("dp", "seq", None), P(), P(), P(None, "seq", None)),
        out_specs=(P("dp", "seq", None), P("dp", "seq", None), P("dp", "seq"), P()),
        check_vma=False,
    )
```

profile of v0, /device:TPU:1, one launch (start us, length us, event | category | flops | bytes accessed | tf_op | source)
XLA Modules:
  0.0 498.2 jit_solution(6452901341456452620)
XLA Ops:
  8.4 6.4 %convolution_convert_fusion.2 = bf16[512,3072]{1,0:T(8,128)(2,1)S(1)} fusion(bf16[1024,3072]{1,0:T(8,128)(2,1)} %param.7, bf16[1,512,1024]{2,1,0:T(8,128)(2,1)S(1)} %copy-done), kind=kOutput, calls=%fused_computation.22 | convolution fusion | flops 3222798336 | bytes 10485760 | tf_op jit(solution)/shard_map/dot_general | solution.py:73
  14.9 5.2 %collective-permute-start = (bf16[1,3072]{1,0:T(2,128)(2,1)S(1)}, bf16[1,3072]{1,0:T(2,128)(2,1)S(1)}, u32[]{:S(2)}, u32[]{:S(2)}) collective-permute-start(bf16[1,3072]{1,0:T(2,128)(2,1)S(1)} %get-tuple-element.12), channel_id=1, source_target_pairs={{0,1},{1,2},{2,3},{3,4},{4,5},{5,6},{6,7},{7,8},{8,9},{9,10},{10,1... | collective-permute-start | bytes 18440 | tf_op jit(solution)/shard_map/ppermute | solution.py:19
  20.1 1.9 collective-permute-start.1
  22.1 3.0 collective-permute-done.1
  25.1 2.5 multiply_add_fusion
  27.6 2.7 copy-done.2
  32.1 2.1 copy.34
  34.2 9.6 %all-to-all-start.2 = ((bf16[1,2,256,1024]{3,1,0,2:T(2,128)(2,1)}), bf16[1,2,256,1024]{3,1,0,2:T(2,128)(2,1)S(1)}, u32[]{:S(2)}, u32[]{:S(2)}) async-start(bf16[1,2,256,1024]{3,1,0,2:T(2,128)(2,1)} %copy.34), calls=%async_computation.2 | async-start | bytes 2097152 | tf_op jit(solution)/shard_map/all_to_all | solution.py:93
  43.8 1.6 reshape.130
  45.4 24.8 %all-to-all-done.2 = bf16[1,2,256,1024]{3,1,0,2:T(2,128)(2,1)S(1)} async-done(((bf16[1,2,256,1024]{3,1,0,2:T(2,128)(2,1)}), bf16[1,2,256,1024]{3,1,0,2:T(2,128)(2,1)S(1)}, u32[]{:S(2)}, u32[]{:S(2)}) %all-to-all-start.2) | async-done | bytes 1048608 | tf_op jit(solution)/shard_map/all_to_all | solution.py:93
  70.6 1.6 copy.47
  72.2 3.8 convolution_convert_fusion
  76.0 2.0 copy.48
  78.1 32.2 %all_to_all.60 = bf16[1,64,8,1024]{3,2,0,1:T(8,128)(2,1)S(1)} all-to-all(bf16[1,64,8,1024]{3,2,0,1:T(8,128)(2,1)S(1)} %bitcast_bitcast_fusion), channel_id=1, replica_groups=mesh['dp'=8,'seq'=32] {'seq'}, dimensions={1} | all-to-all | bytes 2097152 | tf_op jit(solution)/shard_map/all_to_all | solution.py:100
  111.7 2.2 fusion.14
  113.9 2.4 fusion.18
  116.2 3.7 copy.27
  120.0 32.5 %all_to_all.61 = bf16[1,2,256,1024]{3,1,0,2:T(2,128)(2,1)S(1)} all-to-all(bf16[1,2,256,1024]{3,1,0,2:T(2,128)(2,1)} %copy.27), channel_id=1, replica_groups=mesh['dp'=8,'seq'=32] {'seq'}, dimensions={2} | all-to-all | bytes 2097152 | tf_op jit(solution)/shard_map/all_to_all | solution.py:82
  152.8 1.6 copy.45
  154.4 3.2 convolution_convert_fusion.1
  157.5 1.9 copy.46
  159.6 32.4 %all_to_all.62 = bf16[1,64,8,1024]{3,2,0,1:T(8,128)(2,1)S(1)} all-to-all(bf16[1,64,8,1024]{3,2,0,1:T(8,128)(2,1)S(1)} %bitcast_bitcast_fusion.1), channel_id=1, replica_groups=mesh['dp'=8,'seq'=32] {'seq'}, dimensions={1} | all-to-all | bytes 2097152 | tf_op jit(solution)/shard_map/all_to_all | solution.py:89
  193.3 3.2 fusion.13
  196.8 4.1 collective-permute-start.2
  200.9 3.9 collective-permute-start.3
  205.6 12.4 %convolution_bitcast_fusion.2 = f32[1024,3072]{0,1:T(8,128)} fusion(bf16[1,512,1024]{2,1,0:T(8,128)(2,1)S(1)} %copy-done, bf16[1,3072]{1,0:T(2,128)(2,1)S(1)} %collective-permute-done.3, bf16[512,1024]{1,0:T(8,128)(2,1)S(1)} %copy-done.6, bf16[512,1024]{1,0:T(8,128)(2,1)S(1)} %get-tuple-element.14, bf16[512,1024]{1,0:T(8,128)(2,1)S(1)} %copy-done.5, ...), kind=kOutput, calls=%fused_computation.14 | convolution fusion | flops 3265265664 | bytes 16826368 | tf_op jit(solution)/shard_map/dot_general | solution.py:115
  218.3 5.5 %maximum_convert_fusion = f32[514,3072]{1,0:T(8,128)} fusion(bf16[1,3072]{1,0:T(2,128)(2,1)S(1)} %collective-permute-done.1, bf16[512,3072]{1,0:T(8,128)(2,1)} %copy-done.4, bf16[1,3072]{1,0:T(2,128)(2,1)S(1)} %collective-permute-done), kind=kLoop, calls=%fused_computation.23 | loop fusion | flops 9474048 | bytes 9474048 | tf_op jit(solution)/shard_map/convert_element_type | solution.py:110
  223.8 151.0 %reduce-scatter.3.cloned.1.call-done = f32[128,3072]{0,1:T(8,128)} async-done(((f32[1024,3072]{0,1:T(8,128)}), f32[128,3072]{0,1:T(8,128)}) %reduce-scatter.3.cloned.1.call-update) | async-done | bytes 1572880 | tf_op jit(solution)/shard_map/reduce_scatter | solution.py:114
  374.8 9.3 %fusion.9 = (f32[3072]{0:T(1024)S(1)}, f32[3072]{0:T(1024)S(1)}, f32[3072]{0:T(1024)S(1)}) fusion(f32[514,3072]{1,0:T(8,128)} %maximum_convert_fusion, bf16[512,1024]{1,0:T(8,128)(2,1)S(1)} %copy-done.6, bf16[512,1024]{1,0:T(8,128)(2,1)S(1)} %copy-done.8, bf16[512,1024]{1,0:T(8,128)(2,1)S(1)} %copy-done.5), kind=kLoop, calls=%fused_computation.18 | loop fusion | flops 18865152 | bytes 22056960 | tf_op jit(solution)/shard_map/reduce_sum | solution.py:111
  384.2 75.6 %psum.7 = f32[3,3072]{1,0:T(4,128)S(1)} all-reduce(f32[3,3072]{1,0:T(4,128)S(1)} %pad_maximum_fusion.9), channel_id=1, replica_groups=mesh['dp'=8,'seq'=32] {'dp','seq'}, use_global_device_ids=true, to_apply=%region_5.6 | all-reduce | flops 9216 | bytes 73728 | tf_op jit(solution)/shard_map/psum | solution.py:112
  460.4 11.1 %fusion.17 = bf16[1,512,1024]{2,1,0:T(8,128)(2,1)} fusion(bf16[1024,3072]{1,0:T(8,128)(2,1)} %param.7, bf16[1,3072]{1,0:T(2,128)(2,1)S(1)} %collective-permute-done.3, bf16[512,1024]{1,0:T(8,128)(2,1)S(1)} %copy-done.6, bf16[512,1024]{1,0:T(8,128)(2,1)} %copy-done.7, bf16[512,1024]{1,0:T(8,128)(2,1)S(1)} %copy-done.5, ...), kind=kOutput, calls=%fused_computation.47 | convolution fusion | flops 3265789952 | bytes 10534912 | tf_op jit(solution)/shard_map/dot_general | solution.py:108
  471.5 18.4 %reduce-scatter.5.cloned.1.call-done = f32[128,96]{0,1:T(8,128)} async-done(((f32[128,3072]{0,1:T(8,128)}), f32[128,96]{0,1:T(8,128)}) %reduce-scatter.5.cloned.1.call-update) | async-done | bytes 49168 | tf_op jit(solution)/shard_map/reduce_scatter | solution.py:120
  (56 shorter events, 10.1 us)
Async XLA Ops:
  7.2 1.2 copy-start
  7.2 14.8 %copy-start.12 = (f32[3,3072]{1,0:T(4,128)S(1)}, f32[3,3072]{1,0:T(4,128)}, u32[]{:S(2)}) copy-start(f32[3,3072]{1,0:T(4,128)} %param.8) | copy-start | bytes 110596
  14.8 15.8 %copy-start.4 = (bf16[512,3072]{1,0:T(8,128)(2,1)}, bf16[512,3072]{1,0:T(8,128)(2,1)S(1)}, u32[]{:S(2)}) copy-start(bf16[512,3072]{1,0:T(8,128)(2,1)S(1)} %convolution_convert_fusion.2) | copy-start | bytes 9437188
  14.8 15.5 %copy-start.9 = (bf16[1,512,1024]{2,1,0:T(8,128)(2,1)S(1)}, bf16[1,512,1024]{2,1,0:T(8,128)(2,1)}, u32[]{:S(2)}) copy-start(bf16[1,512,1024]{2,1,0:T(8,128)(2,1)} %param.6) | copy-start | bytes 3145732
  14.9 7.2 %collective-permute-start = (bf16[1,3072]{1,0:T(2,128)(2,1)S(1)}, bf16[1,3072]{1,0:T(2,128)(2,1)S(1)}, u32[]{:S(2)}, u32[]{:S(2)}) collective-permute-start(bf16[1,3072]{1,0:T(2,128)(2,1)S(1)} %get-tuple-element.12), channel_id=1, source_target_pairs={{0,1},{1,2},{2,3},{3,4},{4,5},{5,6},{6,7},{7,8},{8,9},{9,10},{10,1... | collective-permute-start | bytes 18440 | tf_op jit(solution)/shard_map/ppermute | solution.py:19
  20.1 5.0 %collective-permute-start.1 = (bf16[1,3072]{1,0:T(2,128)(2,1)S(1)}, bf16[1,3072]{1,0:T(2,128)(2,1)S(1)}, u32[]{:S(2)}, u32[]{:S(2)}) collective-permute-start(bf16[1,3072]{1,0:T(2,128)(2,1)S(1)} %get-tuple-element.13), channel_id=1, source_target_pairs={{1,0},{2,1},{3,2},{4,3},{5,4},{6,5},{7,6},{8,7},{9,8},{10,9},{11,1... | collective-permute-start | bytes 18440 | tf_op jit(solution)/shard_map/ppermute | solution.py:21
  27.6 2.7 copy-start.2
  30.3 13.5 %copy-start.11 = (bf16[64,8,1024]{2,1,0:T(8,128)(2,1)S(1)}, bf16[64,8,1024]{2,1,0:T(8,128)(2,1)}, u32[]{:S(2)}) copy-start(bf16[64,8,1024]{2,1,0:T(8,128)(2,1)} %param.9) | copy-start | bytes 3145732
  34.2 36.1 %all-to-all-start.2 = ((bf16[1,2,256,1024]{3,1,0,2:T(2,128)(2,1)}), bf16[1,2,256,1024]{3,1,0,2:T(2,128)(2,1)S(1)}, u32[]{:S(2)}, u32[]{:S(2)}) async-start(bf16[1,2,256,1024]{3,1,0,2:T(2,128)(2,1)} %copy.34), calls=%async_computation.2 | async-start | bytes 2097152 | tf_op jit(solution)/shard_map/all_to_all | solution.py:93
  43.8 331.0 %reduce-scatter.3.cloned.1.call-start = ((), (), s32[]{:S(2)}) async-start(), calls=%async_computation.6 | async-start | bytes 14155776 | tf_op jit(solution)/shard_map/reduce_scatter | solution.py:114
  70.6 41.0 %slice-start = ((s8[6291456]{0:T(1024)(128)(4,1)}), s8[2097152]{0:T(1024)(128)(4,1)S(1)}, s32[]{:S(2)}) async-start(s8[6291456]{0:T(1024)(128)(4,1)} %bitcast.146), calls=%async_computation.8 | async-start | bytes 4194304
  76.0 35.6 %slice-start.1 = ((s8[6291456]{0:T(1024)(128)(4,1)}), s8[4194304]{0:T(1024)(128)(4,1)S(1)}, s32[]{:S(2)}) async-start(s8[6291456]{0:T(1024)(128)(4,1)} %bitcast.146), calls=%async_computation.9 | async-start | bytes 8388608
  113.9 40.5 %copy-start.3 = (f32[1,64,8192]{2,1,0:T(8,128)S(1)}, f32[1,64,8192]{2,1,0:T(8,128)}, u32[]{:S(2)}) copy-start(f32[1,64,8192]{2,1,0:T(8,128)} %reshape.130) | copy-start | bytes 6291460
  157.5 35.7 %copy-start.10 = (bf16[1,512,1024]{2,1,0:T(8,128)(2,1)S(1)}, bf16[1,512,1024]{2,1,0:T(8,128)(2,1)}, u32[]{:S(2)}) copy-start(bf16[1,512,1024]{2,1,0:T(8,128)(2,1)} %param.6) | copy-start | bytes 3145732
  159.5 37.0 %copy-start.5 = (bf16[512,1024]{1,0:T(8,128)(2,1)S(1)}, bf16[512,1024]{1,0:T(8,128)(2,1)}, u32[]{:S(2)}) copy-start(bf16[512,1024]{1,0:T(8,128)(2,1)} %get-tuple-element.7) | copy-start | bytes 3145732
  159.5 37.0 %copy-start.6 = (bf16[512,1024]{1,0:T(8,128)(2,1)S(1)}, bf16[512,1024]{1,0:T(8,128)(2,1)}, u32[]{:S(2)}) copy-start(bf16[512,1024]{1,0:T(8,128)(2,1)} %get-tuple-element.8) | copy-start | bytes 3145732
  196.5 9.1 %copy-start.7 = (bf16[512,1024]{1,0:T(8,128)(2,1)}, bf16[512,1024]{1,0:T(8,128)(2,1)S(1)}, u32[]{:S(2)}) copy-start(bf16[512,1024]{1,0:T(8,128)(2,1)S(1)} %get-tuple-element.14) | copy-start | bytes 3145732
  196.8 8.0 %collective-permute-start.2 = (bf16[1,3072]{1,0:T(2,128)(2,1)S(1)}, bf16[1,3072]{1,0:T(2,128)(2,1)S(1)}, u32[]{:S(2)}, u32[]{:S(2)}) collective-permute-start(bf16[1,3072]{1,0:T(2,128)(2,1)S(1)} %get-tuple-element.10), channel_id=1, source_target_pairs={{1,0},{2,1},{3,2},{4,3},{5,4},{6,5},{7,6},{8,7},{9,8},{10,9},{11,1... | collective-permute-start | bytes 18440 | tf_op jit(solution)/shard_map/ppermute | solution.py:21
  200.9 4.8 collective-permute-start.3
  218.0 156.8 %copy-start.8 = (bf16[512,1024]{1,0:T(8,128)(2,1)S(1)}, bf16[512,1024]{1,0:T(8,128)(2,1)}, u32[]{:S(2)}) copy-start(bf16[512,1024]{1,0:T(8,128)(2,1)} %copy-done.7) | copy-start | bytes 3145732
  218.0 271.9 %reduce-scatter.5.cloned.1.call-start = ((), (), s32[]{:S(2)}) async-start(), calls=%async_computation.7 | async-start | bytes 1622016 | tf_op jit(solution)/shard_map/reduce_scatter | solution.py:120
  460.4 30.9 %copy-start.1 = (bf16[1,512,1024]{2,1,0:T(8,128)(2,1)S(1)}, bf16[1,512,1024]{2,1,0:T(8,128)(2,1)}, u32[]{:S(2)}) copy-start(bf16[1,512,1024]{2,1,0:T(8,128)(2,1)} %param.5) | copy-start | bytes 3145732
Sparse Core Ops, SparseCore 0:
  218.1 156.5 reduce-scatter.2
  377.4 112.4 reduce-scatter.4
where the time goes:
time: 502 us; the launch traced here: 498 us
  waiting for transfers between devices  198 us (39%)
  blocking collectives  173 us (34%)
  matrix products  43.3 us (9%)
  other arithmetic  25.5 us (5%)
  starting transfers between devices  25 us (5%)
  local copies, waits for them, and re-layouts  19.3 us (4%)
  between operations  14.4 us (3%)
    reduce_scatter x1, waiting for transfers between devices, shards(): lax.psum_scatter(lax.dot_general(rows, du, contract, preferred_element_ty...  151 us
    psum x1, blocking collectives, shards(): taps_grad = lax.psum(local_taps, ('dp', 'seq')) * factor  75.6 us
    all_to_all x1, blocking collectives, shards(): lax.all_to_all(block_section(w.reshape(1, nblocks, BLK, width), table_q),...  32.5 us
    all_to_all x1, blocking collectives, shards(): lax.all_to_all(span_section(columns, filt, table_p), 'seq', split_axis=1,...  32.4 us
    all_to_all x1, blocking collectives, shards(): lax.all_to_all(span_section(grad_cols, filt, table_p), 'seq', split_axis=...  32.2 us
    all_to_all x1, waiting for transfers between devices, shards(): lax.all_to_all(block_section(e4.reshape(1, nblocks, BLK, width), table_q)...  24.8 us
    reduce_scatter x1, waiting for transfers between devices, shards(): lax.psum_scatter(partial_sum, 'seq', scatter_dimension=1, tiled=True)  18.4 us
    dot_general x1, matrix products, shards(): lax.dot_general(rows, du, contract, preferred_element_type=jnp.float32)  12.4 us
  transfers between devices with their start and end apart: 7, of which 5 were waited for; matrix products, arithmetic and copies ran while one was open for 6% of the time, Pallas kernels for 0%

commit v1 on v0

v1 whole, which is shorter than its diff:
```python
import functools
import math

import jax
import jax.numpy as jnp
import numpy as np
from jax import lax
from jax.experimental import pallas as pl
from jax.experimental.pallas import tpu as pltpu
from jax.sharding import PartitionSpec as P

BLK = 256
NC = 4
RT = 64
MESH = pl.DeviceIdType.MESH
F32 = jnp.float32
BF16 = jnp.bfloat16


def dct_table(count):
    rows = np.arange(count, dtype=np.float32)[:, None]
    cols = np.arange(count, dtype=np.float32)[None, :]
    first = np.where(rows == 0, np.float32(math.sqrt(0.5)), np.float32(1.0))
    angle = np.float32(math.pi) * (cols + np.float32(0.5)) * rows / np.float32(count)
    table = np.float32(math.sqrt(2.0 / count)) * first * np.cos(angle.astype(np.float32))
    return table.astype(np.float32)


def tables(nseq, nb):
    share = BLK // nseq
    span = nb * nseq
    size = nb * BLK
    cq = dct_table(BLK)
    cp = dct_table(span)
    first = np.zeros((nseq, nb, share, nb, BLK), np.float32)
    for b in range(nb):
        first[:, b, :, b, :] = cq.reshape(nseq, share, BLK)
    first = first.reshape(size, size)
    second = np.zeros((span, share, span, share), np.float32)
    for r in range(share):
        second[:, r, :, r] = cp
    second = second.reshape(size, size)
    return np.stack([first, second, first.T, second.T]).astype(jnp.bfloat16)


def kernel(
    n,
    x_hbm,
    og_hbm,
    w_hbm,
    taps,
    filt_hbm,
    tab_hbm,
    mixed_hbm,
    ing_hbm,
    wg_hbm,
    tg,
    xv,
    ogv,
    wv,
    fv,
    tab,
    zb,
    sb,
    ub,
    s1,
    r1,
    s2,
    r2,
    hd,
    dsb,
    dub,
    acc,
    mx,
    igb,
    wgb,
    xsem,
    tabsem,
    wsem,
    ogsem,
    fsem,
    hs_sem,
    hr_sem,
    ss1,
    rs1,
    ss2,
    rs2,
    ds_s,
    ds_r,
    mxsem,
    igsem,
    wgsem,
):
    tok, width = x_hbm.shape
    cw = width // NC
    rows2 = r1.shape[2]
    me = lax.axis_index("seq")
    right, left = lax.rem(me + 1, n), lax.rem(me + n - 1, n)

    def cols(g, k):
        return pl.ds(pl.multiple_of(g * width + k * cw, cw), cw)

    xcopy = pltpu.make_async_copy(x_hbm, xv.at[pl.ds(0, tok)], xsem)
    xcopy.start()

    def wcopy(k, g):
        return pltpu.make_async_copy(w_hbm.at[:, cols(g, k)], wv.at[k * 3 + g], wsem.at[k * 3 + g])

    def ogcopy(k):
        return pltpu.make_async_copy(og_hbm.at[:, cols(0, k)], ogv.at[k], ogsem.at[k])

    def fcopy(k):
        return pltpu.make_async_copy(filt_hbm.at[:, cols(0, k)], fv.at[k], fsem.at[k])

    tabcopy = pltpu.make_async_copy(tab_hbm, tab, tabsem)
    for g in range(3):
        wcopy(0, g).start()
    ogcopy(0).start()
    tabcopy.start()

    @pl.loop(1, NC)
    def _(k):
        for g in range(3):
            wcopy(k, g).start()
        ogcopy(k).start()

    @pl.loop(0, NC)
    def _(k):
        fcopy(k).start()

    barrier = pltpu.get_barrier_semaphore()

    @pl.loop(1, n)
    def _(d):
        pl.semaphore_signal(
            barrier, inc=1, device_id={"seq": lax.rem(me + d, n)}, device_id_type=MESH
        )

    xcopy.wait()
    pl.semaphore_wait(barrier, n - 1)

    def xhalo(side):
        src = xv.at[pl.ds(tok - 16, 16)] if side == 0 else xv.at[pl.ds(0, 16)]
        dst = xv.at[pl.ds(tok, 16)] if side == 0 else xv.at[pl.ds(tok + 16, 16)]
        return pltpu.make_async_remote_copy(
            src_ref=src,
            dst_ref=dst,
            send_sem=hs_sem.at[side],
            recv_sem=hr_sem.at[side],
            device_id={"seq": right if side == 0 else left},
            device_id_type=MESH,
        )

    xhalo(0).start()
    xhalo(1).start()
    xhalo(0).wait()
    xhalo(1).wait()
    tabcopy.wait()
    lmask = jnp.where(me == 0, 0.0, 1.0).astype(F32)
    rmask = jnp.where(me == n - 1, 0.0, 1.0).astype(F32)

    def spread(src, dst, ssem, rsem, k):
        @pl.loop(1, n)
        def _(d):
            peer = lax.rem(me + d, n)
            pltpu.make_async_remote_copy(
                src_ref=src.at[k, peer],
                dst_ref=dst.at[k, me],
                send_sem=ssem.at[k],
                recv_sem=rsem.at[k],
                device_id={"seq": peer},
                device_id_type=MESH,
            ).start()

        pltpu.make_async_copy(src.at[k, me], dst.at[k, me], rsem.at[k]).start()

    def arrived(dst, rsem, k):
        pltpu.make_async_copy(dst.at[k], dst.at[k], rsem.at[k]).wait()

    def sent(src, ssem, k):
        part = src.at[k, pl.ds(0, n - 1)]
        pltpu.make_async_copy(part, part, ssem.at[k]).wait()

    def shifted(blk):
        size = RT + 16
        prev = pltpu.roll(blk, 1, 0)[8 : 8 + RT]
        nxt = pltpu.roll(blk, size - 1, 0)[8 : 8 + RT]
        return prev, blk[8 : 8 + RT], nxt

    def stage1(k):
        for g in range(3):
            wcopy(k, g).wait()
            kk = k * 3 + g
            z = jnp.dot(xv[...], wv[kk], preferred_element_type=F32).astype(BF16).astype(F32)
            zb[kk, pl.ds(8, tok), :] = z[:tok]
            zb[kk, pl.ds(0, 8), :] = z[tok + 8 : tok + 16] * lmask
            zb[kk, pl.ds(8 + tok, 8), :] = z[tok + 16 : tok + 24] * rmask
        ogcopy(k).wait()

        @pl.loop(0, tok // RT)
        def _(i):
            base = pl.multiple_of(i * RT, RT)
            parts = []
            for g in range(3):
                kk = k * 3 + g
                prev, here, nxt = shifted(zb[kk, pl.ds(base, RT + 16), :])
                t = taps[:, cols(g, k)]
                s = t[0:1] * prev + t[1:2] * here + t[2:3] * nxt
                sb[kk, pl.ds(base, RT), :] = s
                parts.append(s)
            a, gate, v = parts
            grad = ogv[k, pl.ds(base, RT), :].astype(F32)
            ub[pl.ds(base, RT), pl.ds(0, cw)] = (a * v).astype(BF16)
            ub[pl.ds(base, RT), pl.ds(cw, cw)] = (grad * gate).astype(BF16)

        for h in range(2):
            hc = pl.ds(h * cw, cw)
            h1 = jnp.dot(tab[0], ub[:, hc], preferred_element_type=F32).astype(BF16)
            s1[k, :, :, hc] = h1.reshape(n, rows2, cw)
        spread(s1, r1, ss1, rs1, k)

    def stage2(k):
        arrived(r1, rs1, k)
        fcopy(k).wait()
        for h in range(2):
            hc = pl.ds(h * cw, cw)
            got = r1[k, :, :, hc].reshape(tok, cw)
            h2 = jnp.dot(tab[1], got, preferred_element_type=F32)
            f = (fv[k].astype(F32) * h2).astype(BF16)
            h3 = jnp.dot(tab[3], f, preferred_element_type=F32).astype(BF16)
            s2[k, :, :, hc] = h3.reshape(n, rows2, cw)
        spread(s2, r2, ss2, rs2, k)

    def dshalo(k, side):
        group = pl.ds(k * 3, 3)
        if side == 0:
            src, dst = dsb.at[group, pl.ds(tok, 8)], dsb.at[group, pl.ds(0, 8)]
        else:
            src, dst = dsb.at[group, pl.ds(8, 8)], dsb.at[group, pl.ds(8 + tok, 8)]
        return pltpu.make_async_remote_copy(
            src_ref=src,
            dst_ref=dst,
            send_sem=ds_s.at[k, side],
            recv_sem=ds_r.at[k, side],
            device_id={"seq": right if side == 0 else left},
            device_id_type=MESH,
        )

    def mxcopy(k):
        return pltpu.make_async_copy(mx.at[k], mixed_hbm.at[:, cols(0, k)], mxsem.at[k])

    def stage3(k):
        arrived(r2, rs2, k)
        for h in range(2):
            got = r2[k, :, :, pl.ds(h * cw, cw)].reshape(tok, cw)
            hd[h] = jnp.dot(tab[2], got, preferred_element_type=F32)

        @pl.loop(0, tok // RT)
        def _(i):
            base = pl.multiple_of(i * RT, RT)
            at = pl.ds(base, RT)
            h4, dw = hd[0, at, :], hd[1, at, :]
            a, gate, v = (sb[k * 3 + g, at, :] for g in range(3))
            grad = ogv[k, at, :].astype(F32)
            mx[k, at, :] = (gate * h4).astype(BF16)
            inner = pl.ds(base + 8, RT)
            dsb[k * 3, inner, :] = (dw * v).astype(BF16).astype(F32)
            dsb[k * 3 + 1, inner, :] = (grad * h4).astype(BF16).astype(F32)
            dsb[k * 3 + 2, inner, :] = (dw * a).astype(BF16).astype(F32)

        dshalo(k, 0).start()
        dshalo(k, 1).start()
        mxcopy(k).start()

    def stage4(k):
        dshalo(k, 0).wait()
        dshalo(k, 1).wait()

        @pl.when(me == 0)
        def _():
            dsb[pl.ds(k * 3, 3), pl.ds(0, 8), :] = jnp.zeros((3, 8, cw), F32)

        @pl.when(me == n - 1)
        def _():
            dsb[pl.ds(k * 3, 3), pl.ds(8 + tok, 8), :] = jnp.zeros((3, 8, cw), F32)

        def rows(i, sums):
            base = pl.multiple_of(i * RT, RT)
            out = []
            for g in range(3):
                kk = k * 3 + g
                prev, here, nxt = shifted(dsb[kk, pl.ds(base, RT + 16), :])
                t = taps[:, cols(g, k)]
                du = t[0:1] * nxt + t[1:2] * here + t[2:3] * prev
                dub[g, pl.ds(base, RT), :] = du.astype(BF16)
                for j, z in enumerate(shifted(zb[kk, pl.ds(base, RT + 16), :])):
                    out.append(
                        sums[g * 3 + j] + jnp.sum((here * z).reshape(RT // 8, 8, cw), axis=0)
                    )
            return tuple(out)

        sums = lax.fori_loop(0, tok // RT, rows, tuple(jnp.zeros((8, cw), F32) for _ in range(9)))
        for g in range(3):
            tg[:, cols(g, k)] = jnp.concatenate(
                [jnp.sum(sums[g * 3 + j], axis=0, keepdims=True) for j in range(3)], axis=0
            )

        nt = (((1,), (1,)), ((), ()))
        tn = (((0,), (0,)), ((), ()))

        @pl.loop(0, width // 256)
        def _(j):
            at = pl.ds(pl.multiple_of(j * 256, 256), 256)
            total = jnp.zeros((tok, 256), F32)
            for g in range(3):
                total += lax.dot_general(
                    dub[g], wv[k * 3 + g, at, :], nt, preferred_element_type=F32
                )

            @pl.when(k == 0)
            def _():
                acc[j] = total

            @pl.when(k > 0)
            def _():
                acc[j] += total

            for g in range(3):
                wgb[k * 3 + g, at, :] = lax.dot_general(
                    xv[pl.ds(0, tok), at], dub[g], tn, preferred_element_type=F32
                ).astype(BF16)

        for g in range(3):
            wgcopy(k, g).start()

    def wgcopy(k, g):
        return pltpu.make_async_copy(
            wgb.at[k * 3 + g], wg_hbm.at[:, cols(g, k)], wgsem.at[k * 3 + g]
        )

    @pl.loop(0, NC)
    def _(k):
        stage1(k)

    @pl.loop(0, NC + 2)
    def _(t):
        @pl.when(t < NC)
        def _():
            stage2(t)

        @pl.when((t >= 1) & (t <= NC))
        def _():
            stage3(t - 1)

        @pl.when(t >= 2)
        def _():
            stage4(t - 2)

    igs = []
    for j in range(width // 256):
        at = pl.ds(j * 256, 256)
        igb[:, at] = acc[j].astype(BF16)
        copy = pltpu.make_async_copy(igb.at[:, at], ing_hbm.at[:, at], igsem.at[j])
        copy.start()
        igs.append(copy)

    @pl.loop(0, NC)
    def _(k):
        sent(s1, ss1, k)
        sent(s2, ss2, k)
        mxcopy(k).wait()
        for g in range(3):
            wgcopy(k, g).wait()

    for copy in igs:
        copy.wait()


def fused(rows, grads, w_in, taps, filt, n):
    tok, width = rows.shape
    nb = tok // BLK
    cw = width // NC
    share = BLK // n
    tab = jnp.asarray(tables(n, nb))
    any_space = pl.BlockSpec(memory_space=pl.ANY)
    vmem = pl.BlockSpec(memory_space=pltpu.VMEM)
    dma = pltpu.SemaphoreType.DMA
    return pl.pallas_call(
        functools.partial(kernel, n),
        out_shape=(
            jax.ShapeDtypeStruct((tok, width), BF16),
            jax.ShapeDtypeStruct((tok, width), BF16),
            jax.ShapeDtypeStruct((width, 3 * width), BF16),
            jax.ShapeDtypeStruct((3, 3 * width), F32),
        ),
        in_specs=[any_space, any_space, any_space, vmem, any_space, any_space],
        out_specs=(any_space, any_space, any_space, vmem),
        scratch_shapes=[
            pltpu.VMEM((tok + 32, width), BF16),
            pltpu.VMEM((NC, tok, cw), BF16),
            pltpu.VMEM((3 * NC, width, cw), BF16),
            pltpu.VMEM((NC, tok, cw), BF16),
            pltpu.VMEM((4, tok, tok), BF16),
            pltpu.VMEM((3 * NC, tok + 16, cw), F32),
            pltpu.VMEM((3 * NC, tok, cw), F32),
            pltpu.VMEM((tok, 2 * cw), BF16),
            pltpu.VMEM((NC, n, nb * share, 2 * cw), BF16),
            pltpu.VMEM((NC, n, nb * share, 2 * cw), BF16),
            pltpu.VMEM((NC, n, nb * share, 2 * cw), BF16),
            pltpu.VMEM((NC, n, nb * share, 2 * cw), BF16),
            pltpu.VMEM((2, tok, cw), F32),
            pltpu.VMEM((3 * NC, tok + 16, cw), F32),
            pltpu.VMEM((3, tok, cw), BF16),
            pltpu.VMEM((width // 256, tok, 256), F32),
            pltpu.VMEM((NC, tok, cw), BF16),
            pltpu.VMEM((tok, width), BF16),
            pltpu.VMEM((3 * NC, width, cw), BF16),
            dma,
            dma,
            dma((3 * NC,)),
            dma((NC,)),
            dma((NC,)),
            dma((2,)),
            dma((2,)),
            dma((NC,)),
            dma((NC,)),
            dma((NC,)),
            dma((NC,)),
            dma((NC, 2)),
            dma((NC, 2)),
            dma((NC,)),
            dma((width // 256,)),
            dma((3 * NC,)),
        ],
        compiler_params=pltpu.CompilerParams(
            collective_id=0, has_side_effects=True, vmem_limit_bytes=67043328
        ),
        name="monarch",
    )(rows, grads, w_in, taps, filt.reshape(tok, width), tab)


def shards(inputs, out_grad, w_in, taps, filt):
    tok = inputs.shape[1]
    nseq = lax.axis_size("seq")
    ndata = lax.axis_size("dp")
    factor = 1.0 / math.sqrt(ndata * nseq * tok)
    mixed, in_grad, wg, local_taps = fused(inputs[0], out_grad[0], w_in, taps, filt, nseq)
    taps_grad = lax.psum(local_taps, ("dp", "seq")) * factor
    partial_sum = lax.psum_scatter(wg, "dp", scatter_dimension=0, tiled=True)
    w_grad = lax.psum_scatter(partial_sum, "seq", scatter_dimension=1, tiled=True)
    return (mixed[None], in_grad[None], w_grad.astype(F32) * factor, taps_grad)


def solution(mesh):
    return jax.shard_map(
        shards,
        mesh=mesh,
        in_specs=(P("dp", "seq", None), P("dp", "seq", None), P(), P(), P(None, "seq", None)),
        out_specs=(P("dp", "seq", None), P("dp", "seq", None), P("dp", "seq"), P()),
        check_vma=False,
    )
```

time: 502 us -> 364 us (0.73)
  Pallas kernels: 0 us -> 127 us
  blocking collectives: 173 us -> 76.6 us
  waiting for transfers between devices: 198 us -> 137 us
  matrix products: 43.3 us -> 0 us
  starting transfers between devices: 25 us -> 0.08 us
  other arithmetic: 25.5 us -> 0.64 us
  local copies, waits for them, and re-layouts: 19.3 us -> 5.79 us
    pallas_call x0 -> x1, Pallas kernels: none -> 127 us  [fused(): pl.pallas_call(functools.partial(kernel, n), out_shape=(jax.ShapeDtypeStr...]
    all_to_all x3 -> x0, blocking collectives: 97.1 us -> none  [the longest x1 32.5 us: shards(): lax.all_to_all(block_section(w.reshape(1, nblocks, BLK, width), table_q),...]
    reduce_scatter x2 -> x1, waiting for transfers between devices: 169 us -> 102 us  [shards(): partial_sum = lax.psum_scatter(wg, 'dp', scatter_dimension=0, tiled=True)]
    dot_general x9 -> x0, matrix products: 43.3 us -> none  [the longest x1 12.4 us: shards(): lax.dot_general(rows, du, contract, preferred_element_type=jnp.float32)]
    unnamed x2 -> x3, waiting for transfers between devices: 0.03 us -> 35.5 us
    all_to_all x1 -> x0, waiting for transfers between devices: 24.8 us -> none  [shards(): lax.all_to_all(block_section(e4.reshape(1, nblocks, BLK, width), table_q)...]
    ppermute x4 -> x0, starting transfers between devices: 15.1 us -> none  [the longest x2 9.14 us: padded(): lax.ppermute(tail, axis, [(i, (i + 1) % count) for i in range(ends)])]
    all_to_all x1 -> x0, starting transfers between devices: 9.6 us -> none  [shards(): lax.all_to_all(block_section(e4.reshape(1, nblocks, BLK, width), table_q)...]
  transfers between devices with their start and end apart: 7 -> 2, of which waited for: 5 -> 2; matrix products, arithmetic and copies ran while one was open for 6% -> 0% of each run, Pallas kernels for 0% -> 0%
where the time goes in v1:
time: 364 us; the launch traced here: 361 us
  waiting for transfers between devices  137 us (38%)
  Pallas kernels  127 us (35%)
  blocking collectives  76.6 us (21%)
  between operations  14.1 us (4%)
  local copies, waits for them, and re-layouts  5.79 us (2%)
    pallas_call x1, Pallas kernels, fused(): pl.pallas_call(functools.partial(kernel, n), out_shape=(jax.ShapeDtypeStr...  127 us
    reduce_scatter x1, waiting for transfers between devices, shards(): partial_sum = lax.psum_scatter(wg, 'dp', scatter_dimension=0, tiled=True)  102 us
    psum x1, blocking collectives, shards(): taps_grad = lax.psum(local_taps, ('dp', 'seq')) * factor  76.6 us
    unnamed x3, waiting for transfers between devices  35.5 us
  transfers between devices with their start and end apart: 2, of which 2 were waited for; matrix products, arithmetic and copies ran while one was open for 0% of the time, Pallas kernels for 0%

profile of v1, /device:TPU:1, one launch (start us, length us, event | category | flops | bytes accessed | tf_op | source)
XLA Modules:
  0.0 360.9 jit_solution(7566221174096873757)
XLA Ops:
  7.2 0.0 reduce-scatter.5.cloned.1.call-start
  7.2 126.6 %monarch.1 = (bf16[512,1024]{1,0:T(8,128)(2,1)}, bf16[512,1024]{1,0:T(8,128)(2,1)}, bf16[1024,3072]{1,0:T(8,128)(2,1)}, f32[3,3072]{1,0:T(4,128)}) custom-call(bf16[512,1024]{1,0:T(8,128)(2,1)} %bitcast.10, bf16[512,1024]{1,0:T(8,128)(2,1)} %bitcast.11, bf16[1024,3072]{1,0:T(8,128)(2,1)} %w_hbm.1, f32[3,3072]{1,0:T(4,128)} %taps.1, ...), custom_call_target="tpu_custom_call" | custom-call | tf_op jit(solution)/shard_map/monarch/pallas_call | solution.py:388
  133.8 0.0 copy-start.2
  133.8 0.0 copy-start.1
  133.8 0.0 copy-start
  133.8 0.0 reduce-scatter.5.cloned.1.call-update
  133.8 0.0 reduce-scatter.7.cloned.1.call-start
  133.9 101.6 %reduce-scatter.5.cloned.1.call-done = bf16[128,3072]{1,0:T(8,128)(2,1)} async-done(((bf16[1024,3072]{1,0:T(8,128)(2,1)}), bf16[128,3072]{1,0:T(8,128)(2,1)}) %reduce-scatter.5.cloned.1.call-update) | async-done | bytes 786448 | tf_op jit(solution)/shard_map/reduce_scatter | solution.py:449
  235.5 2.3 copy.12
  237.8 0.0 reduce-scatter.7.cloned.1.call-update
  237.8 0.0 copy-done.2
  237.8 76.6 %psum.7 = f32[3,3072]{1,0:T(4,128)S(1)} all-reduce(f32[3,3072]{1,0:T(4,128)S(1)} %copy-done.2), channel_id=1, replica_groups=mesh['dp'=8,'seq'=32] {'dp','seq'}, use_global_device_ids=true, to_apply=%region_2.0 | all-reduce | flops 9216 | bytes 73728 | tf_op jit(solution)/shard_map/psum | solution.py:448
  314.4 0.6 broadcast_multiply_fusion
  315.0 35.5 %reduce-scatter.7.cloned.1.call-done = bf16[96,128]{1,0:T(8,128)(2,1)} async-done(((bf16[3072,128]{1,0:T(8,128)(2,1)}), bf16[96,128]{1,0:T(8,128)(2,1)}) %reduce-scatter.7.cloned.1.call-update) | async-done | bytes 24592
  350.5 0.8 copy.13
  351.4 0.7 copy.11
  352.1 0.0 copy-done.1
  352.1 1.0 copy.16
  353.1 0.0 copy-done
  353.1 1.0 copy.17
  (1 shorter events, 0.0 us)
Async XLA Ops:
  7.2 228.3 %reduce-scatter.5.cloned.1.call-start = ((), (), s32[]{:S(2)}) async-start(), calls=%async_computation.2 | async-start | bytes 7077888 | tf_op jit(solution)/shard_map/reduce_scatter | solution.py:449
  133.8 104.0 %copy-start.2 = (f32[3,3072]{1,0:T(4,128)S(1)}, f32[3,3072]{1,0:T(4,128)}, u32[]{:S(2)}) copy-start(f32[3,3072]{1,0:T(4,128)} %get-tuple-element.11) | copy-start | bytes 110596
  133.8 218.3 %copy-start.1 = (bf16[512,1024]{1,0:T(8,128)(2,1)S(1)}, bf16[512,1024]{1,0:T(8,128)(2,1)}, u32[]{:S(2)}) copy-start(bf16[512,1024]{1,0:T(8,128)(2,1)} %get-tuple-element.8) | copy-start | bytes 3145732
  133.8 219.3 %copy-start = (bf16[512,1024]{1,0:T(8,128)(2,1)S(1)}, bf16[512,1024]{1,0:T(8,128)(2,1)}, u32[]{:S(2)}) copy-start(bf16[512,1024]{1,0:T(8,128)(2,1)} %get-tuple-element.9) | copy-start | bytes 3145732
  133.8 216.7 %reduce-scatter.7.cloned.1.call-start = ((), (), s32[]{:S(2)}) async-start(), calls=%async_computation.3 | async-start | bytes 811008
Sparse Core Ops, SparseCore 0:
  134.0 101.4 reduce-scatter.4
  238.7 111.7 reduce-scatter.6

commit v2 on v1

--- a/solution.py
+++ b/solution.py
@@ -45,6 +45,8 @@
 
 def kernel(
     n,
+    ndp,
+    factor,
     x_hbm,
     og_hbm,
     w_hbm,
@@ -53,8 +55,8 @@
     tab_hbm,
     mixed_hbm,
     ing_hbm,
-    wg_hbm,
-    tg,
+    wg_out,
+    tg_out,
     xv,
     ogv,
     wv,
@@ -71,9 +73,19 @@
     dsb,
     dub,
     acc,
-    mx,
-    igb,
+    xt,
     wgb,
+    cr,
+    xr,
+    ys,
+    yr,
+    fs,
+    fr,
+    tb,
+    tr,
+    t2s,
+    t2r,
+    t3r,
     xsem,
     tabsem,
     wsem,
@@ -89,13 +101,27 @@
     ds_r,
     mxsem,
     igsem,
-    wgsem,
+    c_s,
+    c_r,
+    x_s,
+    x_r,
+    y_s,
+    y_r,
+    f_s,
+    f_r,
+    t_s,
+    t_r,
 ):
     tok, width = x_hbm.shape
     cw = width // NC
     rows2 = r1.shape[2]
     me = lax.axis_index("seq")
     right, left = lax.rem(me + 1, n), lax.rem(me + n - 1, n)
+    dpi = lax.axis_index("dp")
+    xn = ndp // 2
+    xi, yh = dpi // 2, lax.rem(dpi, 2)
+    core = lax.rem(me, 2)
+    sibling = me + 1 - 2 * core
 
     def cols(g, k):
         return pl.ds(pl.multiple_of(g * width + k * cw, cw), cw)
@@ -136,8 +162,17 @@
             barrier, inc=1, device_id={"seq": lax.rem(me + d, n)}, device_id_type=MESH
         )
 
+    @pl.loop(1, ndp)
+    def _(d):
+        pl.semaphore_signal(
+            barrier, inc=1, device_id={"dp": lax.rem(dpi + d, ndp)}, device_id_type=MESH
+        )
+
     xcopy.wait()
-    pl.semaphore_wait(barrier, n - 1)
+    for c in range(2):
+        for q in range(xn):
+            xt[c, pl.ds(q * 128, 128), :] = xv[pl.ds(0, tok), pl.ds((2 * q + c) * 128, 128)].T
+    pl.semaphore_wait(barrier, n + ndp - 2)
 
     def xhalo(side):
         src = xv.at[pl.ds(tok - 16, 16)] if side == 0 else xv.at[pl.ds(0, 16)]
@@ -247,7 +282,7 @@
         )
 
     def mxcopy(k):
-        return pltpu.make_async_copy(mx.at[k], mixed_hbm.at[:, cols(0, k)], mxsem.at[k])
+        return pltpu.make_async_copy(ogv.at[k], mixed_hbm.at[:, cols(0, k)], mxsem.at[k])
 
     def stage3(k):
         arrived(r2, rs2, k)
@@ -262,7 +297,7 @@
             h4, dw = hd[0, at, :], hd[1, at, :]
             a, gate, v = (sb[k * 3 + g, at, :] for g in range(3))
             grad = ogv[k, at, :].astype(F32)
-            mx[k, at, :] = (gate * h4).astype(BF16)
+            ogv[k, at, :] = (gate * h4).astype(BF16)
             inner = pl.ds(base + 8, RT)
             dsb[k * 3, inner, :] = (dw * v).astype(BF16).astype(F32)
             dsb[k * 3 + 1, inner, :] = (grad * h4).astype(BF16).astype(F32)
@@ -300,13 +335,18 @@
             return tuple(out)
 
         sums = lax.fori_loop(0, tok // RT, rows, tuple(jnp.zeros((8, cw), F32) for _ in range(9)))
+        sums = [jnp.sum(part, axis=0, keepdims=True) for part in sums]
+        packed = jnp.concatenate(sums + [jnp.zeros((7, cw), F32)], axis=0)
+        for q in range(cw // 128):
+            tb[k * (cw // 128) + q] = packed[:, q * 128 : (q + 1) * 128]
+
         for g in range(3):
-            tg[:, cols(g, k)] = jnp.concatenate(
-                [jnp.sum(sums[g * 3 + j], axis=0, keepdims=True) for j in range(3)], axis=0
-            )
+            wgb[k * 3 + g, 1 - core] = jnp.dot(
+                xt[1 - core], dub[g], preferred_element_type=F32
+            ).astype(BF16)
+        ccopy(k).start()
 
         nt = (((1,), (1,)), ((), ()))
-        tn = (((0,), (0,)), ((), ()))
 
         @pl.loop(0, width // 256)
         def _(j):
@@ -325,17 +365,105 @@
             def _():
                 acc[j] += total
 
+        ccopy(k).wait_recv()
+        for g in range(3):
+            own = jnp.dot(xt[core], dub[g], preferred_element_type=F32)
+            wgb[k * 3 + g, core] = (own + cr[k * 3 + g].astype(F32)).astype(BF16)
+        for d in range(1, xn):
+            xcopy_out(k, lax.rem(xi + d, xn)).start()
+
+    def ccopy(k):
+        group = pl.ds(k * 3, 3)
+        return pltpu.make_async_remote_copy(
+            src_ref=wgb.at[group, 1 - core],
+            dst_ref=cr.at[group],
+            send_sem=c_s.at[k],
+            recv_sem=c_r.at[k],
+            device_id={"seq": sibling},
+            device_id_type=MESH,
+        )
+
+    def block(q):
+        return pl.ds(pl.multiple_of(q * 128, 128), 128)
+
+    def xcopy_out(k, q):
+        return pltpu.make_async_remote_copy(
+            src_ref=wgb.at[pl.ds(k * 3, 3), core, block(q)],
+            dst_ref=xr.at[k, xi],
+            send_sem=x_s.at[k],
+            recv_sem=x_r.at[k],
+            device_id={"dp": q * 2 + yh},
+            device_id_type=MESH,
+        )
+
+    def ycopy(k):
+        return pltpu.make_async_remote_copy(
+            src_ref=ys.at[k],
+            dst_ref=yr.at[k],
+            send_sem=y_s.at[k],
+            recv_sem=y_r.at[k],
+            device_id={"dp": xi * 2 + 1 - yh},
+            device_id_type=MESH,
+        )
+
+    def local_wait(ref, sem):
+        pltpu.make_async_copy(ref, ref, sem).wait()
+
+    def stage5(k):
+        local_wait(xr.at[k, pl.ds(0, xn - 1)], x_r.at[k])
+        for g in range(3):
+            total = wgb[k * 3 + g, core, block(xi), :].astype(F32)
+            for d in range(1, xn):
+                total += xr[k, lax.rem(xi + d, xn), g].astype(F32)
+            ys[k, g] = total.astype(BF16)
+
+        @pl.when(yh != core)
+        def _():
+            ycopy(k).start()
+
+    def stage6(k):
+        @pl.when(yh == core)
+        def _():
+            ycopy(k).wait_recv()
             for g in range(3):
-                wgb[k * 3 + g, at, :] = lax.dot_general(
-                    xv[pl.ds(0, tok), at], dub[g], tn, preferred_element_type=F32
-                ).astype(BF16)
-
-        for g in range(3):
-            wgcopy(k, g).start()
-
-    def wgcopy(k, g):
-        return pltpu.make_async_copy(
-            wgb.at[k * 3 + g], wg_hbm.at[:, cols(g, k)], wgsem.at[k * 3 + g]
+                total = ys[k, g].astype(F32) + yr[k, g].astype(F32)
+                fs[pl.ds((k * 3 + g) * (cw // 32), cw // 32)] = (
+                    total.T.astype(BF16).reshape(cw // 32, 32, 128)
+                )
+            for g in range(3):
+
+                @pl.loop(0, cw // 32)
+                def _(i):
+                    piece = (g * width + k * cw) // 32 + i
+                    owner, slot = piece // per, lax.rem(piece, per)
+                    src = fs.at[(k * 3 + g) * (cw // 32) + i]
+                    dst = fr.at[me // 2, slot]
+
+                    @pl.when(owner == me)
+                    def _():
+                        pltpu.make_async_copy(src, dst, f_r).start()
+
+                    @pl.when(owner != me)
+                    def _():
+                        pltpu.make_async_remote_copy(
+                            src_ref=src,
+                            dst_ref=dst,
+                            send_sem=f_s,
+                            recv_sem=f_r,
+                            device_id={"seq": owner},
+                            device_id_type=MESH,
+                        ).start()
+
+    per = fr.shape[1]
+
+    def taps_copy(step, src, dst, axis, peer):
+        return pltpu.make_async_remote_copy(
+            src_ref=src,
+            dst_ref=dst,
+            send_sem=t_s.at[step],
+            recv_sem=t_r.at[step],
+            device_id={axis: peer},
+            device_id_type=MESH,
         )
 
     @pl.loop(0, NC)
@@ -356,45 +484,112 @@
         def _():
             stage4(t - 2)
 
+        @pl.when(t >= 3)
+        def _():
+            stage5(t - 3)
+
+        @pl.when(t >= 4)
+        def _():
+            stage6(t - 4)
+
+    tr[dpi] = tb[dpi]
+
+    @pl.loop(1, ndp)
+    def _(d):
+        peer = lax.rem(dpi + d, ndp)
+        taps_copy(0, tb.at[peer], tr.at[dpi], "dp", peer).start()
+
     igs = []
-    for j in range(width // 256):
-        at = pl.ds(j * 256, 256)
-        igb[:, at] = acc[j].astype(BF16)
-        copy = pltpu.make_async_copy(igb.at[:, at], ing_hbm.at[:, at], igsem.at[j])
+    for j in range(NC):
+        fv[j] = acc[j].astype(BF16)
+        copy = pltpu.make_async_copy(
+            fv.at[j], ing_hbm.at[:, pl.ds(j * cw, cw)], igsem.at[j]
+        )
         copy.start()
         igs.append(copy)
+
+    stage6(NC - 2)
+    stage5(NC - 1)
+
+    local_wait(tr.at[pl.ds(0, ndp - 1)], t_r.at[0])
+    total = tr[0]
+    for m in range(1, ndp):
+        total += tr[m]
+    t2s[...] = total
+
+    @pl.loop(1, n)
+    def _(d):
+        peer = lax.rem(me + d, n)
+        taps_copy(1, t2s, t2r.at[me], "seq", peer).start()
+
+    pltpu.make_async_copy(t2s, t2r.at[me], t_r.at[1]).start()
+    stage6(NC - 1)
+
+    local_wait(t2r, t_r.at[1])
+    t3r[dpi] = lax.fori_loop(0, n, lambda i, c: c + t2r[i], jnp.zeros((16, 128), F32)) * factor
+
+    @pl.loop(1, ndp)
+    def _(d):
+        taps_copy(2, t3r.at[dpi], t3r.at[dpi], "dp", lax.rem(dpi + d, ndp)).start()
+
+    local_wait(fr, f_r)
+    for p in range(per):
+        wg_out[pl.ds(p * 32, 32), :] = (
+            lax.fori_loop(
+                0, n // 2, lambda i, c, p=p: c + fr[i, p].astype(F32), jnp.zeros((32, 128), F32)
+            )
+            * factor
+        )
+
+    local_wait(t3r.at[pl.ds(0, ndp - 1)], t_r.at[2])
+    for m in range(ndp):
+        for g in range(3):
+            tg_out[:, pl.ds(g * width + m * 128, 128)] = t3r[m, pl.ds(g * 3, 3), :]
 
     @pl.loop(0, NC)
     def _(k):
         sent(s1, ss1, k)
         sent(s2, ss2, k)
         mxcopy(k).wait()
-        for g in range(3):
-            wgcopy(k, g).wait()
-
+        ccopy(k).wait_send()
+        local_wait(xr.at[k, pl.ds(0, xn - 1)], x_s.at[k])
+
+        @pl.when(yh != core)
+        def _():
+            ycopy(k).wait_send()
+
+    @pl.when(yh == core)
+    def _():
+        local_wait(fs.at[pl.ds(0, fs.shape[0] - per)], f_s)
+
+    local_wait(tr.at[pl.ds(0, ndp - 1)], t_s.at[0])
+    local_wait(t2r.at[pl.ds(0, n - 1)], t_s.at[1])
+    local_wait(tr.at[pl.ds(0, ndp - 1)], t_s.at[2])
     for copy in igs:
         copy.wait()
 
 
-def fused(rows, grads, w_in, taps, filt, n):
+def fused(rows, grads, w_in, taps, filt, n, ndp, factor):
     tok, width = rows.shape
     nb = tok // BLK
     cw = width // NC
     share = BLK // n
+    per = 3 * width // n // 32
+    assert cw == 256 and width == 128 * ndp and ndp % 2 == 0 and per * 32 * n == 3 * width
     tab = jnp.asarray(tables(n, nb))
     any_space = pl.BlockSpec(memory_space=pl.ANY)
     vmem = pl.BlockSpec(memory_space=pltpu.VMEM)
     dma = pltpu.SemaphoreType.DMA
     return pl.pallas_call(
-        functools.partial(kernel, n),
+        functools.partial(kernel, n, ndp, factor),
         out_shape=(
             jax.ShapeDtypeStruct((tok, width), BF16),
             jax.ShapeDtypeStruct((tok, width), BF16),
-            jax.ShapeDtypeStruct((width, 3 * width), BF16),
+            jax.ShapeDtypeStruct((per * 32, 128), F32),
             jax.ShapeDtypeStruct((3, 3 * width), F32),
         ),
         in_specs=[any_space, any_space, any_space, vmem, any_space, any_space],
-        out_specs=(any_space, any_space, any_space, vmem),
+        out_specs=(any_space, any_space, vmem, vmem),
         scratch_shapes=[
             pltpu.VMEM((tok + 32, width), BF16),
             pltpu.VMEM((NC, tok, cw), BF16),
@@ -412,9 +607,19 @@
             pltpu.VMEM((3 * NC, tok + 16, cw), F32),
             pltpu.VMEM((3, tok, cw), BF16),
             pltpu.VMEM((width // 256, tok, 256), F32),
-            pltpu.VMEM((NC, tok, cw), BF16),
-            pltpu.VMEM((tok, width), BF16),
-            pltpu.VMEM((3 * NC, width, cw), BF16),
+            pltpu.VMEM((2, 64 * ndp, tok), BF16),
+            pltpu.VMEM((3 * NC, 2, 64 * ndp, cw), BF16),
+            pltpu.VMEM((3 * NC, 64 * ndp, cw), BF16),
+            pltpu.VMEM((NC, ndp // 2, 3, 128, cw), BF16),
+            pltpu.VMEM((NC, 3, 128, cw), BF16),
+            pltpu.VMEM((NC, 3, 128, cw), BF16),
+            pltpu.VMEM((per * n, 32, 128), BF16),
+            pltpu.VMEM((n // 2, per, 32, 128), BF16),
+            pltpu.VMEM((ndp, 16, 128), F32),
+            pltpu.VMEM((ndp, 16, 128), F32),
+            pltpu.VMEM((16, 128), F32),
+            pltpu.VMEM((n, 16, 128), F32),
+            pltpu.VMEM((ndp, 16, 128), F32),
             dma,
             dma,
             dma((3 * NC,)),
@@ -429,8 +634,17 @@
             dma((NC, 2)),
             dma((NC, 2)),
             dma((NC,)),
-            dma((width // 256,)),
-            dma((3 * NC,)),
+            dma((NC,)),
+            dma((NC,)),
+            dma((NC,)),
+            dma((NC,)),
+            dma((NC,)),
+            dma((NC,)),
+            dma((NC,)),
+            dma,
+            dma,
+            dma((3,)),
+            dma((3,)),
         ],
         compiler_params=pltpu.CompilerParams(
             collective_id=0, has_side_effects=True, vmem_limit_bytes=67043328
@@ -444,11 +658,10 @@
     nseq = lax.axis_size("seq")
     ndata = lax.axis_size("dp")
     factor = 1.0 / math.sqrt(ndata * nseq * tok)
-    mixed, in_grad, wg, local_taps = fused(inputs[0], out_grad[0], w_in, taps, filt, nseq)
-    taps_grad = lax.psum(local_taps, ("dp", "seq")) * factor
-    partial_sum = lax.psum_scatter(wg, "dp", scatter_dimension=0, tiled=True)
-    w_grad = lax.psum_scatter(partial_sum, "seq", scatter_dimension=1, tiled=True)
-    return (mixed[None], in_grad[None], w_grad.astype(F32) * factor, taps_grad)
+    mixed, in_grad, w_grad, taps_grad = fused(
+        inputs[0], out_grad[0], w_in, taps, filt, nseq, ndata, factor
+    )
+    return (mixed[None], in_grad[None], w_grad.T, taps_grad)
 
 
 def solution(mesh):

time: 364 us -> 162 us (0.45)
  waiting for transfers between devices: 137 us -> 0 us
  blocking collectives: 76.6 us -> 0 us
  Pallas kernels: 127 us -> 154 us
  between operations: 14.1 us -> 0.64 us
    reduce_scatter x1 -> x0, waiting for transfers between devices: 102 us -> none  [shards(): partial_sum = lax.psum_scatter(wg, 'dp', scatter_dimension=0, tiled=True)]
    psum x1 -> x0, blocking collectives: 76.6 us -> none  [shards(): taps_grad = lax.psum(local_taps, ('dp', 'seq')) * factor]
    unnamed x3 -> x0, waiting for transfers between devices: 35.5 us -> none
    pallas_call x1, Pallas kernels: 127 us -> 154 us  [fused(): pl.pallas_call(functools.partial(kernel, n, ndp, factor), out_shape=(jax....]
    unnamed x11 -> x4, local copies, waits for them, and re-layouts: 5.79 us -> 7.37 us
  transfers between devices with their start and end apart: 2 -> 0, of which waited for: 2 -> 0; matrix products, arithmetic and copies ran while one was open for 0% -> 0% of each run, Pallas kernels for 0% -> 0%
where the time goes in v2:
time: 162 us
  Pallas kernels  154 us (95%)
  local copies, waits for them, and re-layouts  7.37 us (5%)
    pallas_call x1, Pallas kernels, fused(): pl.pallas_call(functools.partial(kernel, n, ndp, factor), out_shape=(jax....  154 us
    unnamed x4, local copies, waits for them, and re-layouts  7.37 us

profile of v2, /device:TPU:1, one launch (start us, length us, event | category | flops | bytes accessed | tf_op | source)
XLA Modules:
  0.0 161.9 jit_solution(1620804882389255701)
XLA Ops:
  0.6 153.8 %monarch.1 = (bf16[512,1024]{1,0:T(8,128)(2,1)}, bf16[512,1024]{1,0:T(8,128)(2,1)}, f32[96,128]{1,0:T(8,128)}, f32[3,3072]{1,0:T(4,128)}) custom-call(bf16[512,1024]{1,0:T(8,128)(2,1)} %bitcast.8, bf16[512,1024]{1,0:T(8,128)(2,1)} %bitcast.9, bf16[1024,3072]{1,0:T(8,128)(2,1)} %w_hbm.1, f32[3,3072]{1,0:T(4,128)} %taps.1, bf16[512,1024]{1,0:T(8,128)(2,1)} %bitcast.10, ...), custom_call_target="tpu_custom_call" | custom-call | tf_op jit(solution)/shard_map/monarch/pallas_call | solution.py:583
  154.5 2.3 %copy.14 = bf16[1,512,1024]{2,1,0:T(8,128)(2,1)} copy(bf16[1,512,1024]{2,1,0:T(8,128)(2,1)} %bitcast.7) | data formatting | bytes 2097152
  156.7 2.3 %copy.15 = bf16[1,512,1024]{2,1,0:T(8,128)(2,1)} copy(bf16[1,512,1024]{2,1,0:T(8,128)(2,1)} %bitcast.6) | data formatting | bytes 2097152
  159.0 1.4 copy.16
  160.4 1.4 copy.17

commit v3 on v2

--- a/solution.py
+++ b/solution.py
@@ -188,9 +188,6 @@
 
     xhalo(0).start()
     xhalo(1).start()
-    xhalo(0).wait()
-    xhalo(1).wait()
-    tabcopy.wait()
     lmask = jnp.where(me == 0, 0.0, 1.0).astype(F32)
     rmask = jnp.where(me == n - 1, 0.0, 1.0).astype(F32)
 
@@ -226,10 +223,21 @@
         for g in range(3):
             wcopy(k, g).wait()
             kk = k * 3 + g
-            z = jnp.dot(xv[...], wv[kk], preferred_element_type=F32).astype(BF16).astype(F32)
-            zb[kk, pl.ds(8, tok), :] = z[:tok]
-            zb[kk, pl.ds(0, 8), :] = z[tok + 8 : tok + 16] * lmask
-            zb[kk, pl.ds(8 + tok, 8), :] = z[tok + 16 : tok + 24] * rmask
+            z = jnp.dot(xv[pl.ds(0, tok)], wv[kk], preferred_element_type=F32)
+            zb[kk, pl.ds(8, tok), :] = z.astype(BF16).astype(F32)
+
+        @pl.when(k == 0)
+        def _():
+            xhalo(0).wait()
+            xhalo(1).wait()
+            tabcopy.wait()
+
+        for g in range(3):
+            kk = k * 3 + g
+            z = jnp.dot(xv[pl.ds(tok, 32)], wv[kk], preferred_element_type=F32)
+            z = z.astype(BF16).astype(F32)
+            zb[kk, pl.ds(0, 8), :] = z[8:16] * lmask
+            zb[kk, pl.ds(8 + tok, 8), :] = z[16:24] * rmask
         ogcopy(k).wait()
 
         @pl.loop(0, tok // RT)
@@ -340,11 +348,30 @@
         for q in range(cw // 128):
             tb[k * (cw // 128) + q] = packed[:, q * 128 : (q + 1) * 128]
 
+        @pl.when(k == NC - 1)
+        def _():
+            tr[dpi] = tb[dpi]
+
+            @pl.loop(1, ndp)
+            def _(d):
+                peer = lax.rem(dpi + d, ndp)
+                taps_copy(0, tb.at[peer], tr.at[dpi], "dp", peer).start()
+
         for g in range(3):
             wgb[k * 3 + g, 1 - core] = jnp.dot(
                 xt[1 - core], dub[g], preferred_element_type=F32
             ).astype(BF16)
         ccopy(k).start()
+
+        half = pl.ds(0, 64 * ndp)
+        for g in range(3):
+            zb[k * 3 + g, half, :] = jnp.dot(xt[core], dub[g], preferred_element_type=F32)
+        ccopy(k).wait_recv()
+        for g in range(3):
+            kk = k * 3 + g
+            wgb[kk, core] = (zb[kk, half, :] + cr[kk].astype(F32)).astype(BF16)
+        for d in range(1, xn):
+            xcopy_out(k, lax.rem(xi + d, xn)).start()
 
         nt = (((1,), (1,)), ((), ()))
 
@@ -364,13 +391,6 @@
             @pl.when(k > 0)
             def _():
                 acc[j] += total
-
-        ccopy(k).wait_recv()
-        for g in range(3):
-            own = jnp.dot(xt[core], dub[g], preferred_element_type=F32)
-            wgb[k * 3 + g, core] = (own + cr[k * 3 + g].astype(F32)).astype(BF16)
-        for d in range(1, xn):
-            xcopy_out(k, lax.rem(xi + d, xn)).start()
 
     def ccopy(k):
         group = pl.ds(k * 3, 3)
@@ -470,34 +490,27 @@
     def _(k):
         stage1(k)
 
-    @pl.loop(0, NC + 2)
+    @pl.loop(0, NC)
+    def _(k):
+        stage2(k)
+
+    @pl.loop(0, NC + 1)
     def _(t):
+        @pl.when(t >= 2)
+        def _():
+            stage5(t - 2)
+
+        @pl.when(t >= 3)
+        def _():
+            stage6(t - 3)
+
+        @pl.when(t >= 1)
+        def _():
+            stage4(t - 1)
+
         @pl.when(t < NC)
         def _():
-            stage2(t)
-
-        @pl.when((t >= 1) & (t <= NC))
-        def _():
-            stage3(t - 1)
-
-        @pl.when(t >= 2)
-        def _():
-            stage4(t - 2)
-
-        @pl.when(t >= 3)
-        def _():
-            stage5(t - 3)
-
-        @pl.when(t >= 4)
-        def _():
-            stage6(t - 4)
-
-    tr[dpi] = tb[dpi]
-
-    @pl.loop(1, ndp)
-    def _(d):
-        peer = lax.rem(dpi + d, ndp)
-        taps_copy(0, tb.at[peer], tr.at[dpi], "dp", peer).start()
+            stage3(t)
 
     igs = []
     for j in range(NC):
@@ -509,7 +522,6 @@
         igs.append(copy)
 
     stage6(NC - 2)
-    stage5(NC - 1)
 
     local_wait(tr.at[pl.ds(0, ndp - 1)], t_r.at[0])
     total = tr[0]
@@ -523,7 +535,7 @@
         taps_copy(1, t2s, t2r.at[me], "seq", peer).start()
 
     pltpu.make_async_copy(t2s, t2r.at[me], t_r.at[1]).start()
-    stage6(NC - 1)
+    stage5(NC - 1)
 
     local_wait(t2r, t_r.at[1])
     t3r[dpi] = lax.fori_loop(0, n, lambda i, c: c + t2r[i], jnp.zeros((16, 128), F32)) * factor
@@ -531,6 +543,8 @@
     @pl.loop(1, ndp)
     def _(d):
         taps_copy(2, t3r.at[dpi], t3r.at[dpi], "dp", lax.rem(dpi + d, ndp)).start()
+
+    stage6(NC - 1)
 
     local_wait(fr, f_r)
     for p in range(per):
@@ -653,6 +667,52 @@
     )(rows, grads, w_in, taps, filt.reshape(tok, width), tab)
 
 
+def finish_kernel(mixed, ing, wg, tg, mixed_out, ing_out, wg_out, tg_out, buf, isem, osem):
+    parts = isem.shape[1]
+    size = mixed.shape[0] // parts
+
+    def move(a, j, src, dst, sem):
+        return pltpu.make_async_copy(src, dst, sem.at[a, j])
+
+    def fetch(a, j):
+        at = pl.ds(j * size, size)
+        return move(a, j, (mixed, ing)[a].at[at], buf.at[a, at], isem)
+
+    def put(a, j):
+        at = pl.ds(j * size, size)
+        return move(a, j, buf.at[a, at], (mixed_out, ing_out)[a].at[at], osem)
+
+    pieces = [(a, j) for j in range(parts) for a in range(2)]
+    for piece in pieces:
+        fetch(*piece).start()
+    wg_out[...] = wg[...]
+    tg_out[...] = tg[...]
+    for piece in pieces:
+        fetch(*piece).wait()
+        put(*piece).start()
+    for piece in pieces:
+        put(*piece).wait()
+
+
+def finish(mixed, ing, wg, tg):
+    any_space = pl.BlockSpec(memory_space=pl.ANY)
+    vmem = pl.BlockSpec(memory_space=pltpu.VMEM)
+    dma = pltpu.SemaphoreType.DMA((2, 4))
+    return pl.pallas_call(
+        finish_kernel,
+        out_shape=(
+            jax.ShapeDtypeStruct(mixed.shape, mixed.dtype),
+            jax.ShapeDtypeStruct(ing.shape, ing.dtype),
+            jax.ShapeDtypeStruct(wg.shape, wg.dtype),
+            jax.ShapeDtypeStruct(tg.shape, tg.dtype),
+        ),
+        in_specs=[any_space, any_space, vmem, vmem],
+        out_specs=(any_space, any_space, vmem, vmem),
+        scratch_shapes=[pltpu.VMEM((2, *mixed.shape), mixed.dtype), dma, dma],
+        name="finish",
+    )(mixed, ing, wg, tg)
+
+
 def shards(inputs, out_grad, w_in, taps, filt):
     tok = inputs.shape[1]
     nseq = lax.axis_size("seq")
@@ -661,6 +721,7 @@
     mixed, in_grad, w_grad, taps_grad = fused(
         inputs[0], out_grad[0], w_in, taps, filt, nseq, ndata, factor
     )
+    mixed, in_grad, w_grad, taps_grad = finish(mixed, in_grad, w_grad, taps_grad)
     return (mixed[None], in_grad[None], w_grad.T, taps_grad)
 
 

time: 162 us -> 185 us (1.14)
  Pallas kernels: 154 us -> 183 us
  local copies, waits for them, and re-layouts: 7.37 us -> 0 us
    pallas_call x1, Pallas kernels: 154 us -> 179 us  [fused(): pl.pallas_call(functools.partial(kernel, n, ndp, factor), out_shape=(jax....]
    unnamed x4 -> x0, local copies, waits for them, and re-layouts: 7.37 us -> none
    pallas_call x0 -> x1, Pallas kernels: none -> 3.85 us  [finish(): pl.pallas_call(finish_kernel, out_shape=(jax.ShapeDtypeStruct(mixed.shape...]
where the time goes in v3:
time: 185 us; the launch traced here: 184 us
  Pallas kernels  183 us (99%)
    pallas_call x1, Pallas kernels, fused(): pl.pallas_call(functools.partial(kernel, n, ndp, factor), out_shape=(jax....  179 us
    pallas_call x1, Pallas kernels, finish(): pl.pallas_call(finish_kernel, out_shape=(jax.ShapeDtypeStruct(mixed.shape...  3.85 us

profile of v3, /device:TPU:1, one launch (start us, length us, event | category | flops | bytes accessed | tf_op | source)
XLA Modules:
  0.0 183.6 jit_solution(16448538011673871809)
XLA Ops:
  0.6 179.1 %monarch.1 = (bf16[512,1024]{1,0:T(8,128)(2,1)}, bf16[512,1024]{1,0:T(8,128)(2,1)}, f32[96,128]{1,0:T(8,128)}, f32[3,3072]{1,0:T(4,128)}) custom-call(bf16[512,1024]{1,0:T(8,128)(2,1)} %bitcast.6, bf16[512,1024]{1,0:T(8,128)(2,1)} %bitcast.7, bf16[1024,3072]{1,0:T(8,128)(2,1)} %w_hbm.1, f32[3,3072]{1,0:T(4,128)} %taps.1, bf16[512,1024]{1,0:T(8,128)(2,1)} %bitcast.8, ...), custom_call_target="tpu_custom_call" | custom-call | tf_op jit(solution)/shard_map/monarch/pallas_call | solution.py:597
  179.7 3.9 %finish.1 = (bf16[512,1024]{1,0:T(8,128)(2,1)}, bf16[512,1024]{1,0:T(8,128)(2,1)}, f32[96,128]{1,0:T(8,128)}, f32[3,3072]{1,0:T(4,128)}) custom-call(bf16[512,1024]{1,0:T(8,128)(2,1)} %get-tuple-element.12.mixed, bf16[512,1024]{1,0:T(8,128)(2,1)} %get-tuple-element.13.ing, f32[96,128]{1,0:T(8,128)} %get-tuple-element.14.wg, f32[3,3072]{1,0:T(4,128)} %get-tuple-element.15.tg), custom_call_target="tpu_custom_call" | custom-call | tf_op jit(solution)/shard_map/finish/pallas_call | solution.py:701

commit v4 on v2

--- a/solution.py
+++ b/solution.py
@@ -509,7 +509,6 @@
         igs.append(copy)
 
     stage6(NC - 2)
-    stage5(NC - 1)
 
     local_wait(tr.at[pl.ds(0, ndp - 1)], t_r.at[0])
     total = tr[0]
@@ -523,6 +522,7 @@
         taps_copy(1, t2s, t2r.at[me], "seq", peer).start()
 
     pltpu.make_async_copy(t2s, t2r.at[me], t_r.at[1]).start()
+    stage5(NC - 1)
     stage6(NC - 1)
 
     local_wait(t2r, t_r.at[1])
@@ -653,6 +653,52 @@
     )(rows, grads, w_in, taps, filt.reshape(tok, width), tab)
 
 
+def finish_kernel(mixed, ing, wg, tg, mixed_out, ing_out, wg_out, tg_out, buf, isem, osem):
+    parts = isem.shape[1]
+    size = mixed.shape[0] // parts
+
+    def move(a, j, src, dst, sem):
+        return pltpu.make_async_copy(src, dst, sem.at[a, j])
+
+    def fetch(a, j):
+        at = pl.ds(j * size, size)
+        return move(a, j, (mixed, ing)[a].at[at], buf.at[a, at], isem)
+
+    def put(a, j):
+        at = pl.ds(j * size, size)
+        return move(a, j, buf.at[a, at], (mixed_out, ing_out)[a].at[at], osem)
+
+    pieces = [(a, j) for j in range(parts) for a in range(2)]
+    for piece in pieces:
+        fetch(*piece).start()
+    wg_out[...] = wg[...]
+    tg_out[...] = tg[...]
+    for piece in pieces:
+        fetch(*piece).wait()
+        put(*piece).start()
+    for piece in pieces:
+        put(*piece).wait()
+
+
+def finish(mixed, ing, wg, tg):
+    any_space = pl.BlockSpec(memory_space=pl.ANY)
+    vmem = pl.BlockSpec(memory_space=pltpu.VMEM)
+    dma = pltpu.SemaphoreType.DMA((2, 4))
+    return pl.pallas_call(
+        finish_kernel,
+        out_shape=(
+            jax.ShapeDtypeStruct(mixed.shape, mixed.dtype),
+            jax.ShapeDtypeStruct(ing.shape, ing.dtype),
+            jax.ShapeDtypeStruct(wg.shape, wg.dtype),
+            jax.ShapeDtypeStruct(tg.shape, tg.dtype),
+        ),
+        in_specs=[any_space, any_space, vmem, vmem],
+        out_specs=(any_space, any_space, vmem, vmem),
+        scratch_shapes=[pltpu.VMEM((2, *mixed.shape), mixed.dtype), dma, dma],
+        name="finish",
+    )(mixed, ing, wg, tg)
+
+
 def shards(inputs, out_grad, w_in, taps, filt):
     tok = inputs.shape[1]
     nseq = lax.axis_size("seq")
@@ -661,6 +707,7 @@
     mixed, in_grad, w_grad, taps_grad = fused(
         inputs[0], out_grad[0], w_in, taps, filt, nseq, ndata, factor
     )
+    mixed, in_grad, w_grad, taps_grad = finish(mixed, in_grad, w_grad, taps_grad)
     return (mixed[None], in_grad[None], w_grad.T, taps_grad)
 
 

time: 162 us -> 158 us (0.975)
  local copies, waits for them, and re-layouts: 7.37 us -> 0 us
  Pallas kernels: 154 us -> 157 us
    unnamed x4 -> x0, local copies, waits for them, and re-layouts: 7.37 us -> none
    pallas_call x0 -> x1, Pallas kernels: none -> 3.85 us  [finish(): pl.pallas_call(finish_kernel, out_shape=(jax.ShapeDtypeStruct(mixed.shape...]
where the time goes in v4:
time: 158 us
  Pallas kernels  157 us (99%)
    pallas_call x1, Pallas kernels, fused(): pl.pallas_call(functools.partial(kernel, n, ndp, factor), out_shape=(jax....  154 us
    pallas_call x1, Pallas kernels, finish(): pl.pallas_call(finish_kernel, out_shape=(jax.ShapeDtypeStruct(mixed.shape...  3.85 us

profile of v4, /device:TPU:1, one launch (start us, length us, event | category | flops | bytes accessed | tf_op | source)
XLA Modules:
  0.0 158.1 jit_solution(5804854329600426706)
XLA Ops:
  0.6 153.6 %monarch.1 = (bf16[512,1024]{1,0:T(8,128)(2,1)}, bf16[512,1024]{1,0:T(8,128)(2,1)}, f32[96,128]{1,0:T(8,128)}, f32[3,3072]{1,0:T(4,128)}) custom-call(bf16[512,1024]{1,0:T(8,128)(2,1)} %bitcast.6, bf16[512,1024]{1,0:T(8,128)(2,1)} %bitcast.7, bf16[1024,3072]{1,0:T(8,128)(2,1)} %w_hbm.1, f32[3,3072]{1,0:T(4,128)} %taps.1, bf16[512,1024]{1,0:T(8,128)(2,1)} %bitcast.8, ...), custom_call_target="tpu_custom_call" | custom-call | tf_op jit(solution)/shard_map/monarch/pallas_call | solution.py:583
  154.2 3.9 %finish.1 = (bf16[512,1024]{1,0:T(8,128)(2,1)}, bf16[512,1024]{1,0:T(8,128)(2,1)}, f32[96,128]{1,0:T(8,128)}, f32[3,3072]{1,0:T(4,128)}) custom-call(bf16[512,1024]{1,0:T(8,128)(2,1)} %get-tuple-element.12.mixed, bf16[512,1024]{1,0:T(8,128)(2,1)} %get-tuple-element.13.ing, f32[96,128]{1,0:T(8,128)} %get-tuple-element.14.wg, f32[3,3072]{1,0:T(4,128)} %get-tuple-element.15.tg), custom_call_target="tpu_custom_call" | custom-call | tf_op jit(solution)/shard_map/finish/pallas_call | solution.py:687

commit v5 on v4

--- a/solution.py
+++ b/solution.py
@@ -476,13 +476,13 @@
         def _():
             stage2(t)
 
+        @pl.when(t >= 2)
+        def _():
+            stage4(t - 2)
+
         @pl.when((t >= 1) & (t <= NC))
         def _():
             stage3(t - 1)
-
-        @pl.when(t >= 2)
-        def _():
-            stage4(t - 2)
 
         @pl.when(t >= 3)
         def _():

time: 158 us -> 157 us (level)
  no operation moved by 1% of the time
where the time goes in v5:
time: 157 us
  Pallas kernels  156 us (99%)
    pallas_call x1, Pallas kernels, fused(): pl.pallas_call(functools.partial(kernel, n, ndp, factor), out_shape=(jax....  152 us
    pallas_call x1, Pallas kernels, finish(): pl.pallas_call(finish_kernel, out_shape=(jax.ShapeDtypeStruct(mixed.shape...  3.85 us

profile of v5, /device:TPU:1, one launch (start us, length us, event | category | flops | bytes accessed | tf_op | source)
XLA Modules:
  0.0 156.8 jit_solution(3423969832944268893)
XLA Ops:
  0.6 152.4 %monarch.1 = (bf16[512,1024]{1,0:T(8,128)(2,1)}, bf16[512,1024]{1,0:T(8,128)(2,1)}, f32[96,128]{1,0:T(8,128)}, f32[3,3072]{1,0:T(4,128)}) custom-call(bf16[512,1024]{1,0:T(8,128)(2,1)} %bitcast.6, bf16[512,1024]{1,0:T(8,128)(2,1)} %bitcast.7, bf16[1024,3072]{1,0:T(8,128)(2,1)} %w_hbm.1, f32[3,3072]{1,0:T(4,128)} %taps.1, bf16[512,1024]{1,0:T(8,128)(2,1)} %bitcast.8, ...), custom_call_target="tpu_custom_call" | custom-call | tf_op jit(solution)/shard_map/monarch/pallas_call | solution.py:583
  153.0 3.9 %finish.1 = (bf16[512,1024]{1,0:T(8,128)(2,1)}, bf16[512,1024]{1,0:T(8,128)(2,1)}, f32[96,128]{1,0:T(8,128)}, f32[3,3072]{1,0:T(4,128)}) custom-call(bf16[512,1024]{1,0:T(8,128)(2,1)} %get-tuple-element.12.mixed, bf16[512,1024]{1,0:T(8,128)(2,1)} %get-tuple-element.13.ing, f32[96,128]{1,0:T(8,128)} %get-tuple-element.14.wg, f32[3,3072]{1,0:T(4,128)} %get-tuple-element.15.tg), custom_call_target="tpu_custom_call" | custom-call | tf_op jit(solution)/shard_map/finish/pallas_call | solution.py:687
